TPU v7x, 256 devices: a whole 4x4x8 slice. The times are simulated.
256 devices in a mesh: shard: 64 (over z, x_lo, y), blk: 4 (over x_hi, core).
Axes of the slice: x: 4 (x_hi: 2, x_lo: 2; x = x_hi * 2 + x_lo), y: 4, z: 8, core: 2. Of those that a mesh axis runs over, the one named last changes fastest.
Arguments:
- embeddings: bfloat16 [65536, 1024], P(('shard', 'blk')), may hold values from -6 to 6
- doc_cluster: int32 [65536], P(('shard', 'blk')), may hold values from 0 to 255, as said below
- doc_valid: int32 [65536], P(('shard', 'blk')), may hold values 0 or 1
Outputs:
- max_similar: float32 [65536], P(('shard', 'blk'))
Inputs may be any that keep to these rules, and one draw needn't show every extreme that they name: `doc_cluster`: among the documents of one device at most 16 have clusters of one owner group (cluster mod 64), and at most 4 have clusters c of one owner group with one value of (c // 64) mod 4; one owner group, the same on every device, gets exactly 16 from every device, 4 for each such value.
All inputs are finite; a program needn't handle non-finite values. No bound on the sum of `doc_valid` on one device may be relied on, other than what follows from the above.
Results may differ from a plain program's by a relative error of at most 0.00036.
Values may be sent and summed in bfloat16 or wider, within the bound.
A program may use at most 64 MiB of HBM per device.

v0:
```python
import math
import jax
import jax.numpy as jnp
from jax import lax
from jax.sharding import PartitionSpec as P


def unit_rows(embeddings):
    values = embeddings.astype(jnp.float32)
    scale = lax.rsqrt(jnp.mean(values * values, axis=1, keepdims=True) + 1e-05) / math.sqrt(
        values.shape[1]
    )
    return (values * scale).astype(jnp.bfloat16)


def scores_max(rows_query, keys_query, ids_query, rows_other, keys_other, ids_other, key_block):
    query_count = rows_query.shape[0]
    block_rows = 512

    def one_block(block):
        rows_part, keys_part, ids_part = block
        best = jnp.full((rows_part.shape[0],), -1.0, jnp.float32)
        for number in range(rows_other.shape[0] // key_block):
            first = number * key_block
            rows_key = rows_other[first : first + key_block]
            keys_key = keys_other[first : first + key_block]
            ids_key = ids_other[first : first + key_block]
            similar = lax.dot_general(
                rows_part, rows_key, (((1,), (1,)), ((), ())), preferred_element_type=jnp.float32
            )
            same_group = (
                (keys_part[:, None] == keys_key[None, :])
                & (keys_part[:, None] >= 0)
                & (ids_part[:, None] != ids_key[None, :])
            )
            best = jnp.maximum(best, jnp.max(jnp.where(same_group, similar, -1.0), axis=1))
        return best

    stacked = (
        rows_query.reshape(query_count // block_rows, block_rows, -1),
        keys_query.reshape(query_count // block_rows, block_rows),
        ids_query.reshape(query_count // block_rows, block_rows),
    )
    return lax.map(one_block, stacked).reshape(query_count)


def slot_numbers(target, targets, per_target):
    one_hot = (target[:, None] == jnp.arange(targets, dtype=jnp.int32)[None, :]).astype(jnp.int32)
    ranks = jnp.sum((jnp.cumsum(one_hot, axis=0) - 1) * one_hot, axis=1)
    return target * per_target + ranks


def per_device(embeddings, doc_cluster, doc_valid):
    dev_rows, width = embeddings.shape
    shards = lax.axis_size("shard")
    blocks = lax.axis_size("blk")
    capacity = max(blocks, 4 * dev_rows // shards)
    slots = shards * capacity
    device = lax.axis_index("shard") * blocks + lax.axis_index("blk")
    doc_ids = device * dev_rows + jnp.arange(dev_rows, dtype=jnp.int32)
    owner = doc_cluster % shards
    slot_of = slot_numbers(owner, shards, capacity)
    keyed = jnp.where(doc_valid > 0, doc_cluster, -1)
    flat_rows = jnp.zeros((slots, width), jnp.bfloat16).at[slot_of].set(unit_rows(embeddings))
    flat_keys = jnp.full((slots,), -1, jnp.int32).at[slot_of].set(keyed)
    flat_ids = jnp.full((slots,), -1, jnp.int32).at[slot_of].set(doc_ids)
    send_rows = flat_rows.reshape(shards, capacity, width)
    send_keys = flat_keys.reshape(shards, capacity)
    send_ids = flat_ids.reshape(shards, capacity)
    got_rows, got_keys, got_ids = (
        lax.all_to_all(send_rows, "shard", split_axis=0, concat_axis=0, tiled=True),
        lax.all_to_all(send_keys, "shard", split_axis=0, concat_axis=0, tiled=True),
        lax.all_to_all(send_ids, "shard", split_axis=0, concat_axis=0, tiled=True),
    )
    query_rows = got_rows.reshape(slots, width)
    query_keys = got_keys.reshape(slots)
    query_ids = got_ids.reshape(slots)
    best = jnp.maximum(
        jnp.full((slots,), -1.0, jnp.float32),
        scores_max(
            query_rows,
            query_keys,
            query_ids,
            lax.all_gather(query_rows, "blk", axis=0, tiled=True),
            lax.all_gather(query_keys, "blk", axis=0, tiled=True),
            lax.all_gather(query_ids, "blk", axis=0, tiled=True),
            slots,
        ),
    )
    verdict = lax.all_to_all(
        best.reshape(shards, capacity), "shard", split_axis=0, concat_axis=0, tiled=True
    )
    return verdict.reshape(slots)[slot_of]


def solution(mesh):
    placed = (P(("shard", "blk"), None), P(("shard", "blk")), P(("shard", "blk")))
    return jax.shard_map(
        per_device, mesh=mesh, in_specs=placed, out_specs=P(("shard", "blk")), check_vma=False
    )
```

profile of v0, /device:TPU:1, one launch (start us, length us, event | category | flops | bytes accessed | tf_op | source)
XLA Modules:
  0.0 188.0 jit_solution(3267887966830044788)
XLA Ops:
  6.5 0.0 all-gather.2.cloned.1.call-start
  6.5 0.7 compare_select_fusion.3
  7.3 0.6 reduce-window.6
  7.9 0.2 slice_reduce_fusion
  8.1 0.1 fusion.35
  8.2 1.2 fusion.28
  9.5 2.9 %scatter_custom_fusion.2 = bf16[1024,1024]{1,0:T(8,128)(2,1)S(1)} fusion(s32[256]{0:T(256)S(1)} %get-tuple-element.80, bf16[]{:T(256)} %constant.32.clone.1, bf16[256,1024]{1,0:T(8,128)(2,1)} %param.5, f32[256]{0:T(256)S(1)} %rsqrt_multiply_fusion), kind=kCustom, calls=%fused_computation.36 | custom fusion | flops 786432 | bytes 2622466 | tf_op jit(solution)/shard_map/scatter | solution.py:64
  12.4 61.9 %all_to_all.29 = bf16[64,16,1024]{2,1,0:T(8,128)(2,1)} all-to-all(bf16[64,16,1024]{2,1,0:T(8,128)(2,1)S(1)} %bitcast.52), channel_id=1, replica_groups=mesh['shard'=64,'blk'=4] {'shard'}, dimensions={0} | all-to-all | bytes 4194304 | tf_op jit(solution)/shard_map/all_to_all | solution.py:71
  74.3 0.0 all-gather.2.cloned.1.call-update
  74.3 1.4 scatter_custom_fusion.1
  75.7 0.7 all_to_all.21
  76.4 7.6 %all-to-all-start.1 = ((s32[64,1,16]{2,1,0:T(1,128)}), s32[64,1,16]{2,1,0:T(1,128)S(1)}, u32[]{:S(2)}, u32[]{:S(2)}) async-start(s32[64,1,16]{2,1,0:T(1,128)} %bitcast.7), calls=%async_computation.1 | async-start | bytes 65536 | tf_op jit(solution)/shard_map/all_to_all | solution.py:73
  84.1 1.4 scatter_custom_fusion
  85.5 0.7 all_to_all.19
  86.2 7.2 %all-to-all-done.1 = s32[64,1,16]{2,1,0:T(1,128)S(1)} async-done(((s32[64,1,16]{2,1,0:T(1,128)}), s32[64,1,16]{2,1,0:T(1,128)S(1)}, u32[]{:S(2)}, u32[]{:S(2)}) %all-to-all-start.1) | async-done | bytes 4128 | tf_op jit(solution)/shard_map/all_to_all | solution.py:73
  93.4 4.6 %all-to-all-start = ((s32[64,1,16]{2,1,0:T(1,128)}), s32[64,1,16]{2,1,0:T(1,128)S(1)}, u32[]{:S(2)}, u32[]{:S(2)}) async-start(s32[64,1,16]{2,1,0:T(1,128)} %bitcast.6), calls=%async_computation | async-start | bytes 65536 | tf_op jit(solution)/shard_map/all_to_all | solution.py:72
  98.0 0.6 broadcast.127
  98.5 0.7 reduce.16
  99.3 0.1 reshape_reshape.10
  99.4 0.1 reshape.127
  99.5 7.8 %all-to-all-done = s32[64,1,16]{2,1,0:T(1,128)S(1)} async-done(((s32[64,1,16]{2,1,0:T(1,128)}), s32[64,1,16]{2,1,0:T(1,128)S(1)}, u32[]{:S(2)}, u32[]{:S(2)}) %all-to-all-start) | async-done | bytes 4128 | tf_op jit(solution)/shard_map/all_to_all | solution.py:72
  107.2 0.7 reduce.15
  108.0 0.1 reshape_reshape.9
  108.1 0.1 reshape.126
  108.1 10.9 %all_gather.10 = s32[4096]{0:T(1024)S(1)} all-gather(s32[1024]{0:T(1024)S(1)} %reshape.127), channel_id=1, replica_groups=mesh['shard'=64,'blk'=4] {'blk'}, dimensions={0}, use_global_device_ids=true | all-gather | bytes 20480 | tf_op jit(solution)/shard_map/all_gather | solution.py:86
  119.0 6.9 %all_gather.9 = s32[4096]{0:T(1024)S(1)} all-gather(s32[1024]{0:T(1024)S(1)} %reshape.126), channel_id=1, replica_groups=mesh['shard'=64,'blk'=4] {'blk'}, dimensions={0}, use_global_device_ids=true | all-gather | bytes 20480 | tf_op jit(solution)/shard_map/all_gather | solution.py:85
  125.9 14.1 %all-gather.2.cloned.1.call-done = bf16[4096,1024]{1,0:T(8,128)(2,1)} async-done(((bf16[1024,1024]{1,0:T(8,128)(2,1)}), bf16[4096,1024]{1,0:T(8,128)(2,1)}) %all-gather.2.cloned.1.call-update) | async-done | bytes 8388624 | tf_op jit(solution)/shard_map/all_gather | solution.py:84
  140.0 0.0 copy-done
  140.1 17.7 %while.10 = (s32[]{:T(128)}, f32[2,512]{1,0:T(2,128)S(1)}, s32[2,512]{1,0:T(2,128)S(1)}, s32[4096]{0:T(1024)S(1)}, s32[2,512]{1,0:T(2,128)S(1)}, /*index=5*/s32[...) while((s32[]{:T(128)}, f32[2,512]{1,0:T(2,128)S(1)}, ...), condition=%wide.region_12.13_spmd, body=%wide.region_7.12_spmd.sunk | while | flops 4307550720 | bytes 46288020 | solution.py:44
  140.1 0.0 copy-start.1
  140.1 3.3 %select_reduce_fusion.11 = f32[512]{0:T(512)S(1)} fusion(bf16[4096,1024]{1,0:T(8,128)(2,1)} %get-tuple-element.178, s32[1024]{0:T(1024)S(1)} %get-tuple-element.149, s32[1024]{0:T(1024)S(1)} %get-tuple-element.150, pred[512]{0:T(512)(128)(4,1)S(1)} %broadcast_compare_fusion.2, s32[512]{0:T(512)S(1)} %bitcast.61, s32[512]{0:T(512)S(1)} %bitcast.56, ...), kind=kOutput, calls=%fused_computation.13.clone.1 | convolution fusion | flops 1076887040 | bytes 3161088 | tf_op jit(solution)/shard_map/while/body/eval_jaxpr/dot_general | solution.py:28
  143.4 0.7 copy-done.1
  144.1 1.6 select_reduce_fusion.10
  145.7 1.6 select_reduce_fusion.9
  147.3 1.6 select_reduce_fusion.8
  149.0 0.0 copy-start.1
  149.0 3.3 %select_reduce_fusion.11 = f32[512]{0:T(512)S(1)} fusion(bf16[4096,1024]{1,0:T(8,128)(2,1)} %get-tuple-element.178, s32[1024]{0:T(1024)S(1)} %get-tuple-element.149, s32[1024]{0:T(1024)S(1)} %get-tuple-element.150, pred[512]{0:T(512)(128)(4,1)S(1)} %broadcast_compare_fusion.2, s32[512]{0:T(512)S(1)} %bitcast.61, s32[512]{0:T(512)S(1)} %bitcast.56, ...), kind=kOutput, calls=%fused_computation.13.clone.1 | convolution fusion | flops 1076887040 | bytes 3161088 | tf_op jit(solution)/shard_map/while/body/eval_jaxpr/dot_general | solution.py:28
  152.3 0.7 copy-done.1
  153.0 1.6 select_reduce_fusion.10
  154.6 1.6 select_reduce_fusion.9
  156.1 1.6 select_reduce_fusion.8
  157.8 0.7 max_broadcast_in_dim.15
  158.5 10.1 %all-to-all-start.3 = ((f32[64,1,16]{2,1,0:T(1,128)}), f32[64,1,16]{2,1,0:T(1,128)S(1)}, u32[]{:S(2)}, u32[]{:S(2)}) async-start(f32[64,1,16]{2,1,0:T(1,128)} %bitcast.11), calls=%async_computation.3 | async-start | bytes 65536 | tf_op jit(solution)/shard_map/all_to_all | solution.py:90
  168.6 9.3 %all-to-all-done.3 = f32[64,1,16]{2,1,0:T(1,128)S(1)} async-done(((f32[64,1,16]{2,1,0:T(1,128)}), f32[64,1,16]{2,1,0:T(1,128)S(1)}, u32[]{:S(2)}, u32[]{:S(2)}) %all-to-all-start.3) | async-done | bytes 4128 | tf_op jit(solution)/shard_map/all_to_all | solution.py:90
  177.9 0.5 broadcast.129
  178.4 0.7 reduce.17
  179.2 0.1 reshape.130
  179.3 1.9 %gather_fusion = f32[256]{0:T(256)} fusion(f32[1024]{0:T(1024)S(1)} %reshape.130, s32[1024]{0:T(1024)S(1)} %pad_clamp_fusion), kind=kCustom, calls=%fused_computation | custom fusion | bytes 3072 | tf_op jit(solution)/shard_map/gather | solution.py:93
  (19 shorter events, 0.2 us)
Async XLA Ops:
  6.5 133.5 %all-gather.2.cloned.1.call-start = ((), (), s32[]{:S(2)}) async-start(), calls=%async_computation.4 | async-start | bytes 10485760 | tf_op jit(solution)/shard_map/all_gather | solution.py:84
  74.3 65.7 %copy-start = (bf16[64,16,1024]{2,1,0:T(8,128)(2,1)S(1)}, bf16[64,16,1024]{2,1,0:T(8,128)(2,1)}, u32[]{:S(2)}) copy-start(bf16[64,16,1024]{2,1,0:T(8,128)(2,1)} %all_to_all.29) | copy-start | bytes 6291460
  76.4 16.9 %all-to-all-start.1 = ((s32[64,1,16]{2,1,0:T(1,128)}), s32[64,1,16]{2,1,0:T(1,128)S(1)}, u32[]{:S(2)}, u32[]{:S(2)}) async-start(s32[64,1,16]{2,1,0:T(1,128)} %bitcast.7), calls=%async_computation.1 | async-start | bytes 65536 | tf_op jit(solution)/shard_map/all_to_all | solution.py:73
  93.4 13.9 %all-to-all-start = ((s32[64,1,16]{2,1,0:T(1,128)}), s32[64,1,16]{2,1,0:T(1,128)S(1)}, u32[]{:S(2)}, u32[]{:S(2)}) async-start(s32[64,1,16]{2,1,0:T(1,128)} %bitcast.6), calls=%async_computation | async-start | bytes 65536 | tf_op jit(solution)/shard_map/all_to_all | solution.py:72
  140.1 4.0 %copy-start.1 = (bf16[4096,1024]{1,0:T(8,128)(2,1)S(1)}, bf16[4096,1024]{1,0:T(8,128)(2,1)}, u32[]{:S(2)}) copy-start(bf16[4096,1024]{1,0:T(8,128)(2,1)} %get-tuple-element.178) | copy-start | bytes 25165828 | tf_op jit(solution)/shard_map/while
  149.0 4.0 %copy-start.1 = (bf16[4096,1024]{1,0:T(8,128)(2,1)S(1)}, bf16[4096,1024]{1,0:T(8,128)(2,1)}, u32[]{:S(2)}) copy-start(bf16[4096,1024]{1,0:T(8,128)(2,1)} %get-tuple-element.178) | copy-start | bytes 25165828 | tf_op jit(solution)/shard_map/while
  158.5 19.5 %all-to-all-start.3 = ((f32[64,1,16]{2,1,0:T(1,128)}), f32[64,1,16]{2,1,0:T(1,128)S(1)}, u32[]{:S(2)}, u32[]{:S(2)}) async-start(f32[64,1,16]{2,1,0:T(1,128)} %bitcast.11), calls=%async_computation.3 | async-start | bytes 65536 | tf_op jit(solution)/shard_map/all_to_all | solution.py:90
Sparse Core Ops, SparseCore 0:
  74.5 65.5 all-gather.1
where the time goes:
time: 188 us
  blocking collectives  79.7 us (42%)
  waiting for transfers between devices  38.4 us (20%)
  starting transfers between devices  22.3 us (12%)
  matrix products  16.1 us (9%)
  between operations  13.5 us (7%)
  local copies, waits for them, and re-layouts  9.96 us (5%)
  other arithmetic  7.88 us (4%)
    all_to_all x1, blocking collectives, per_device(): lax.all_to_all(send_rows, 'shard', split_axis=0, concat_axis=0, tiled=True)  61.9 us
    dot_general x8, matrix products, one_block(): lax.dot_general(rows_part, rows_key, (((1,), (1,)), ((), ())), preferred_...  16.1 us
    all_gather x1, waiting for transfers between devices, per_device(): lax.all_gather(query_rows, 'blk', axis=0, tiled=True)  14.1 us
    all_gather x1, blocking collectives, per_device(): lax.all_gather(query_ids, 'blk', axis=0, tiled=True)  10.9 us
    all_to_all x1, starting transfers between devices, per_device(): lax.all_to_all(best.reshape(shards, capacity), 'shard', split_axis=0, con...  10.1 us
    all_to_all x1, waiting for transfers between devices, per_device(): lax.all_to_all(best.reshape(shards, capacity), 'shard', split_axis=0, con...  9.32 us
    all_to_all x1, waiting for transfers between devices, per_device(): lax.all_to_all(send_keys, 'shard', split_axis=0, concat_axis=0, tiled=True)  7.76 us
    all_to_all x1, starting transfers between devices, per_device(): lax.all_to_all(send_ids, 'shard', split_axis=0, concat_axis=0, tiled=True)  7.63 us
  transfers between devices with their start and end apart: 4, of which 4 were waited for; matrix products, arithmetic and copies ran while one was open for 3% of the time, Pallas kernels for 0%

commit v1 on v0

--- a/solution.py
+++ b/solution.py
@@ -3,6 +3,13 @@
 import jax.numpy as jnp
 from jax import lax
 from jax.sharding import PartitionSpec as P
+
+
+def gather_over(x, name, dim):
+    peers = lax.axis_size(name)
+    pieces = jnp.stack([x for _ in range(peers)])
+    pieces = lax.all_to_all(pieces, name, split_axis=0, concat_axis=0)
+    return jnp.concatenate(pieces, axis=dim)
 
 
 def unit_rows(embeddings):
@@ -81,7 +88,7 @@
             query_rows,
             query_keys,
             query_ids,
-            lax.all_gather(query_rows, "blk", axis=0, tiled=True),
+            gather_over(query_rows, "blk", 0),
             lax.all_gather(query_keys, "blk", axis=0, tiled=True),
             lax.all_gather(query_ids, "blk", axis=0, tiled=True),
             slots,

time: 188 us -> 256 us (1.36)
  blocking collectives: 79.7 us -> 152 us
  waiting for transfers between devices: 38.4 us -> 20.6 us
  between operations: 13.5 us -> 0.12 us
  starting transfers between devices: 22.3 us -> 35.4 us
  matrix products: 16.1 us -> 25.2 us
  local copies, waits for them, and re-layouts: 9.96 us -> 12.8 us
    all_gather x1, blocking collectives: 10.9 us -> 93.3 us  [per_device(): lax.all_gather(query_ids, 'blk', axis=0, tiled=True)]
    all_gather x1 -> x0, waiting for transfers between devices: 14.1 us -> none  [per_device(): lax.all_gather(query_rows, 'blk', axis=0, tiled=True)]
    all_to_all x0 -> x1, starting transfers between devices: none -> 10.6 us  [gather_over(): pieces = lax.all_to_all(pieces, name, split_axis=0, concat_axis=0)]
    all_to_all x1, blocking collectives: 61.9 us -> 51.7 us  [per_device(): lax.all_to_all(send_rows, 'shard', split_axis=0, concat_axis=0, tiled=True)]
    dot_general x8, matrix products: 16.1 us -> 25.2 us  [one_block(): lax.dot_general(rows_part, rows_key, (((1,), (1,)), ((), ())), preferred_...]
    all_to_all x1, starting transfers between devices: 7.63 us -> 13.6 us  [per_device(): lax.all_to_all(send_ids, 'shard', split_axis=0, concat_axis=0, tiled=True)]
    another operation x1 -> x2, local copies, waits for them, and re-layouts: 0.01 us -> 4.32 us  [the longest x1 4.31 us: gather_over(): pieces = jnp.stack([x for _ in range(peers)])]
    all_to_all x1, starting transfers between devices: 10.1 us -> 6.52 us  [per_device(): lax.all_to_all(best.reshape(shards, capacity), 'shard', split_axis=0, con...]
  transfers between devices with their start and end apart: 4 -> 4, of which waited for: 4 -> 3; matrix products, arithmetic and copies ran while one was open for 3% -> 3% of each run, Pallas kernels for 0% -> 0%
where the time goes in v1:
time: 256 us; the launch traced here: 255 us
  blocking collectives  152 us (59%)
  starting transfers between devices  35.4 us (14%)
  matrix products  25.2 us (10%)
  waiting for transfers between devices  20.6 us (8%)
  local copies, waits for them, and re-layouts  12.8 us (5%)
  other arithmetic  8.59 us (3%)
    all_gather x1, blocking collectives, per_device(): lax.all_gather(query_ids, 'blk', axis=0, tiled=True)  93.3 us
    all_to_all x1, blocking collectives, per_device(): lax.all_to_all(send_rows, 'shard', split_axis=0, concat_axis=0, tiled=True)  51.7 us
    dot_general x8, matrix products, one_block(): lax.dot_general(rows_part, rows_key, (((1,), (1,)), ((), ())), preferred_...  25.2 us
    all_to_all x1, starting transfers between devices, per_device(): lax.all_to_all(send_ids, 'shard', split_axis=0, concat_axis=0, tiled=True)  13.6 us
    all_to_all x1, starting transfers between devices, gather_over(): pieces = lax.all_to_all(pieces, name, split_axis=0, concat_axis=0)  10.6 us
    all_to_all x1, waiting for transfers between devices, per_device(): lax.all_to_all(best.reshape(shards, capacity), 'shard', split_axis=0, con...  9.31 us
    all_gather x1, blocking collectives, per_device(): lax.all_gather(query_keys, 'blk', axis=0, tiled=True)  6.85 us
    all_to_all x1, starting transfers between devices, per_device(): lax.all_to_all(best.reshape(shards, capacity), 'shard', split_axis=0, con...  6.52 us
  transfers between devices with their start and end apart: 4, of which 3 were waited for; matrix products, arithmetic and copies ran while one was open for 3% of the time, Pallas kernels for 0%

profile of v1, /device:TPU:1, one launch (start us, length us, event | category | flops | bytes accessed | tf_op | source)
XLA Modules:
  0.0 254.7 jit_solution(6590088186813413441)
XLA Ops:
  0.0 0.7 compare_select_fusion.3
  0.7 0.6 reduce-window.6
  1.3 0.2 slice_reduce_fusion
  1.6 0.1 fusion.35
  1.7 1.4 scatter_custom_fusion.1
  3.1 0.7 all_to_all.24
  3.8 13.6 %all-to-all-start.1 = ((s32[64,1,16]{2,1,0:T(1,128)}), s32[64,1,16]{2,1,0:T(1,128)S(1)}, u32[]{:S(2)}, u32[]{:S(2)}) async-start(s32[64,1,16]{2,1,0:T(1,128)} %bitcast.7), calls=%async_computation.1 | async-start | bytes 65536 | tf_op jit(solution)/shard_map/all_to_all | solution.py:80
  17.4 1.2 fusion.28
  18.6 1.4 scatter_custom_fusion
  20.0 0.7 all_to_all.22
  20.7 6.0 %all-to-all-done.1 = s32[64,1,16]{2,1,0:T(1,128)S(1)} async-done(((s32[64,1,16]{2,1,0:T(1,128)}), s32[64,1,16]{2,1,0:T(1,128)S(1)}, u32[]{:S(2)}, u32[]{:S(2)}) %all-to-all-start.1) | async-done | bytes 4128 | tf_op jit(solution)/shard_map/all_to_all | solution.py:80
  26.6 4.7 %all-to-all-start = ((s32[64,1,16]{2,1,0:T(1,128)}), s32[64,1,16]{2,1,0:T(1,128)S(1)}, u32[]{:S(2)}, u32[]{:S(2)}) async-start(s32[64,1,16]{2,1,0:T(1,128)} %bitcast.6), calls=%async_computation | async-start | bytes 65536 | tf_op jit(solution)/shard_map/all_to_all | solution.py:79
  31.4 3.8 %scatter_custom_fusion.2 = bf16[1024,1024]{1,0:T(8,128)(2,1)} fusion(s32[256]{0:T(256)S(1)} %get-tuple-element.80, bf16[]{:T(256)} %constant.32.clone.1, bf16[256,1024]{1,0:T(8,128)(2,1)} %param.5, f32[256]{0:T(256)S(1)} %rsqrt_multiply_fusion), kind=kCustom, calls=%fused_computation.36 | custom fusion | flops 786432 | bytes 2622466 | tf_op jit(solution)/shard_map/scatter | solution.py:71
  35.2 5.4 %all-to-all-done = s32[64,1,16]{2,1,0:T(1,128)S(1)} async-done(((s32[64,1,16]{2,1,0:T(1,128)}), s32[64,1,16]{2,1,0:T(1,128)S(1)}, u32[]{:S(2)}, u32[]{:S(2)}) %all-to-all-start) | async-done | bytes 4128 | tf_op jit(solution)/shard_map/all_to_all | solution.py:79
  40.5 51.7 %all_to_all.34 = bf16[64,16,1024]{2,1,0:T(8,128)(2,1)S(1)} all-to-all(bf16[64,16,1024]{2,1,0:T(8,128)(2,1)} %bitcast.53), channel_id=1, replica_groups=mesh['shard'=64,'blk'=4] {'shard'}, dimensions={0} | all-to-all | bytes 4194304 | tf_op jit(solution)/shard_map/all_to_all | solution.py:78
  92.3 4.3 %stack.3 = bf16[4,1024,1024]{2,1,0:T(8,128)(2,1)} broadcast(bf16[1024,1024]{1,0:T(8,128)(2,1)S(1)} %bitcast.51), dimensions={1,2} | broadcast | bytes 10485760 | tf_op jit(solution)/shard_map/stack | solution.py:10
  96.6 10.6 %all-to-all-start.3 = ((bf16[4,1024,1024]{2,1,0:T(8,128)(2,1)}), bf16[4,1024,1024]{2,1,0:T(8,128)(2,1)}, u32[]{:S(2)}, u32[]{:S(2)}) async-start(bf16[4,1024,1024]{2,1,0:T(8,128)(2,1)} %stack.3), calls=%async_computation.3 | async-start | bytes 16777216 | tf_op jit(solution)/shard_map/all_to_all | solution.py:11
  107.2 0.5 broadcast.128
  107.7 0.6 reduce.16
  108.3 0.1 reshape_reshape.10
  108.4 0.1 reshape.129
  108.5 0.6 reduce.15
  109.1 0.1 reshape_reshape.9
  109.2 0.1 reshape.128
  109.3 93.3 %all_gather.7 = s32[4096]{0:T(1024)S(1)} all-gather(s32[1024]{0:T(1024)S(1)} %reshape.129), channel_id=1, replica_groups=mesh['shard'=64,'blk'=4] {'blk'}, dimensions={0}, use_global_device_ids=true | all-gather | bytes 20480 | tf_op jit(solution)/shard_map/all_gather | solution.py:93
  202.6 6.9 %all_gather.6 = s32[4096]{0:T(1024)S(1)} all-gather(s32[1024]{0:T(1024)S(1)} %reshape.128), channel_id=1, replica_groups=mesh['shard'=64,'blk'=4] {'blk'}, dimensions={0}, use_global_device_ids=true | all-gather | bytes 20480 | tf_op jit(solution)/shard_map/all_gather | solution.py:92
  209.4 0.0 all-to-all-done.3
  209.4 25.5 %while.10 = (s32[]{:T(128)}, f32[2,512]{1,0:T(2,128)S(1)}, s32[2,512]{1,0:T(2,128)S(1)}, s32[4096]{0:T(1024)S(1)}, s32[2,512]{1,0:T(2,128)S(1)}, /*index=5*/s32[...) while((s32[]{:T(128)}, f32[2,512]{1,0:T(2,128)S(1)}, ...), condition=%wide.region_12.13_spmd, body=%wide.region_7.12_spmd.sunk | while | flops 4307550720 | bytes 12735085 | solution.py:51
  209.5 3.2 %select_reduce_fusion.11 = f32[512]{0:T(512)S(1)} fusion(bf16[4096,1024]{1,0:T(8,128)(2,1)} %get-tuple-element.178, s32[1024]{0:T(1024)S(1)} %get-tuple-element.149, s32[1024]{0:T(1024)S(1)} %get-tuple-element.150, pred[512]{0:T(512)(128)(4,1)S(1)} %broadcast_compare_fusion.2, s32[512]{0:T(512)S(1)} %bitcast.62, s32[512]{0:T(512)S(1)} %bitcast.57, ...), kind=kOutput, calls=%fused_computation.13.clone.1 | convolution fusion | flops 1076887040 | bytes 3161088 | tf_op jit(solution)/shard_map/while/body/eval_jaxpr/dot_general | solution.py:35
  212.6 3.1 %select_reduce_fusion.10 = f32[512]{0:T(512)S(1)} fusion(bf16[4096,1024]{1,0:T(8,128)(2,1)} %get-tuple-element.178, s32[1024]{0:T(1024)S(1)} %get-tuple-element.147, s32[1024]{0:T(1024)S(1)} %get-tuple-element.148, pred[512]{0:T(512)(128)(4,1)S(1)} %broadcast_compare_fusion.2, s32[512]{0:T(512)S(1)} %bitcast.63, s32[512]{0:T(512)S(1)} %bitcast.58, ...), kind=kOutput, calls=%fused_computation.10.clone.1 | convolution fusion | flops 1076887040 | bytes 3161088 | tf_op jit(solution)/shard_map/while/body/eval_jaxpr/dot_general | solution.py:35
  215.8 3.2 %select_reduce_fusion.9 = f32[512]{0:T(512)S(1)} fusion(bf16[4096,1024]{1,0:T(8,128)(2,1)} %get-tuple-element.178, s32[1024]{0:T(1024)S(1)} %get-tuple-element.145, s32[1024]{0:T(1024)S(1)} %get-tuple-element.146, pred[512]{0:T(512)(128)(4,1)S(1)} %broadcast_compare_fusion.2, s32[512]{0:T(512)S(1)} %bitcast.64, s32[512]{0:T(512)S(1)} %bitcast.59, ...), kind=kOutput, calls=%fused_computation.7.clone.1 | convolution fusion | flops 1076887040 | bytes 3161088 | tf_op jit(solution)/shard_map/while/body/eval_jaxpr/dot_general | solution.py:35
  219.0 3.2 %select_reduce_fusion.8 = f32[512]{0:T(512)S(1)} fusion(bf16[4096,1024]{1,0:T(8,128)(2,1)} %get-tuple-element.178, s32[1024]{0:T(1024)S(1)} %get-tuple-element.141, s32[1024]{0:T(1024)S(1)} %get-tuple-element.142, pred[512]{0:T(512)(128)(4,1)S(1)} %broadcast_compare_fusion.2, s32[512]{0:T(512)S(1)} %bitcast.65, s32[512]{0:T(512)S(1)} %bitcast.60, ...), kind=kOutput, calls=%fused_computation.4.clone.1 | convolution fusion | flops 1076887040 | bytes 3161088 | tf_op jit(solution)/shard_map/while/body/eval_jaxpr/dot_general | solution.py:35
  222.2 3.2 %select_reduce_fusion.11 = f32[512]{0:T(512)S(1)} fusion(bf16[4096,1024]{1,0:T(8,128)(2,1)} %get-tuple-element.178, s32[1024]{0:T(1024)S(1)} %get-tuple-element.149, s32[1024]{0:T(1024)S(1)} %get-tuple-element.150, pred[512]{0:T(512)(128)(4,1)S(1)} %broadcast_compare_fusion.2, s32[512]{0:T(512)S(1)} %bitcast.62, s32[512]{0:T(512)S(1)} %bitcast.57, ...), kind=kOutput, calls=%fused_computation.13.clone.1 | convolution fusion | flops 1076887040 | bytes 3161088 | tf_op jit(solution)/shard_map/while/body/eval_jaxpr/dot_general | solution.py:35
  225.4 3.2 %select_reduce_fusion.10 = f32[512]{0:T(512)S(1)} fusion(bf16[4096,1024]{1,0:T(8,128)(2,1)} %get-tuple-element.178, s32[1024]{0:T(1024)S(1)} %get-tuple-element.147, s32[1024]{0:T(1024)S(1)} %get-tuple-element.148, pred[512]{0:T(512)(128)(4,1)S(1)} %broadcast_compare_fusion.2, s32[512]{0:T(512)S(1)} %bitcast.63, s32[512]{0:T(512)S(1)} %bitcast.58, ...), kind=kOutput, calls=%fused_computation.10.clone.1 | convolution fusion | flops 1076887040 | bytes 3161088 | tf_op jit(solution)/shard_map/while/body/eval_jaxpr/dot_general | solution.py:35
  228.5 3.2 %select_reduce_fusion.9 = f32[512]{0:T(512)S(1)} fusion(bf16[4096,1024]{1,0:T(8,128)(2,1)} %get-tuple-element.178, s32[1024]{0:T(1024)S(1)} %get-tuple-element.145, s32[1024]{0:T(1024)S(1)} %get-tuple-element.146, pred[512]{0:T(512)(128)(4,1)S(1)} %broadcast_compare_fusion.2, s32[512]{0:T(512)S(1)} %bitcast.64, s32[512]{0:T(512)S(1)} %bitcast.59, ...), kind=kOutput, calls=%fused_computation.7.clone.1 | convolution fusion | flops 1076887040 | bytes 3161088 | tf_op jit(solution)/shard_map/while/body/eval_jaxpr/dot_general | solution.py:35
  231.7 3.2 %select_reduce_fusion.8 = f32[512]{0:T(512)S(1)} fusion(bf16[4096,1024]{1,0:T(8,128)(2,1)} %get-tuple-element.178, s32[1024]{0:T(1024)S(1)} %get-tuple-element.141, s32[1024]{0:T(1024)S(1)} %get-tuple-element.142, pred[512]{0:T(512)(128)(4,1)S(1)} %broadcast_compare_fusion.2, s32[512]{0:T(512)S(1)} %bitcast.65, s32[512]{0:T(512)S(1)} %bitcast.60, ...), kind=kOutput, calls=%fused_computation.4.clone.1 | convolution fusion | flops 1076887040 | bytes 3161088 | tf_op jit(solution)/shard_map/while/body/eval_jaxpr/dot_general | solution.py:35
  234.9 0.7 max_broadcast_in_dim.15
  235.6 6.5 %all-to-all-start.4 = ((f32[64,1,16]{2,1,0:T(1,128)}), f32[64,1,16]{2,1,0:T(1,128)S(1)}, u32[]{:S(2)}, u32[]{:S(2)}) async-start(f32[64,1,16]{2,1,0:T(1,128)} %bitcast.12), calls=%async_computation.4 | async-start | bytes 65536 | tf_op jit(solution)/shard_map/all_to_all | solution.py:97
  242.2 9.3 %all-to-all-done.4 = f32[64,1,16]{2,1,0:T(1,128)S(1)} async-done(((f32[64,1,16]{2,1,0:T(1,128)}), f32[64,1,16]{2,1,0:T(1,128)S(1)}, u32[]{:S(2)}, u32[]{:S(2)}) %all-to-all-start.4) | async-done | bytes 4128 | tf_op jit(solution)/shard_map/all_to_all | solution.py:97
  251.5 0.5 broadcast.130
  252.0 0.7 reduce.17
  252.7 0.1 reshape.132
  252.8 1.9 gather_fusion
  (18 shorter events, 0.2 us)
Async XLA Ops:
  3.8 22.9 %all-to-all-start.1 = ((s32[64,1,16]{2,1,0:T(1,128)}), s32[64,1,16]{2,1,0:T(1,128)S(1)}, u32[]{:S(2)}, u32[]{:S(2)}) async-start(s32[64,1,16]{2,1,0:T(1,128)} %bitcast.7), calls=%async_computation.1 | async-start | bytes 65536 | tf_op jit(solution)/shard_map/all_to_all | solution.py:80
  26.6 13.9 %all-to-all-start = ((s32[64,1,16]{2,1,0:T(1,128)}), s32[64,1,16]{2,1,0:T(1,128)S(1)}, u32[]{:S(2)}, u32[]{:S(2)}) async-start(s32[64,1,16]{2,1,0:T(1,128)} %bitcast.6), calls=%async_computation | async-start | bytes 65536 | tf_op jit(solution)/shard_map/all_to_all | solution.py:79
  96.6 112.9 %all-to-all-start.3 = ((bf16[4,1024,1024]{2,1,0:T(8,128)(2,1)}), bf16[4,1024,1024]{2,1,0:T(8,128)(2,1)}, u32[]{:S(2)}, u32[]{:S(2)}) async-start(bf16[4,1024,1024]{2,1,0:T(8,128)(2,1)} %stack.3), calls=%async_computation.3 | async-start | bytes 16777216 | tf_op jit(solution)/shard_map/all_to_all | solution.py:11
  235.6 15.9 %all-to-all-start.4 = ((f32[64,1,16]{2,1,0:T(1,128)}), f32[64,1,16]{2,1,0:T(1,128)S(1)}, u32[]{:S(2)}, u32[]{:S(2)}) async-start(f32[64,1,16]{2,1,0:T(1,128)} %bitcast.12), calls=%async_computation.4 | async-start | bytes 65536 | tf_op jit(solution)/shard_map/all_to_all | solution.py:97
